TPU v7x, 32 devices: a whole 2x2x4 slice. The times are simulated.
32 devices in a mesh: row: 8 (over z, core), rep: 4 (over y, x).
Axes of the slice: x: 2, y: 2, z: 4, core: 2. Of those that a mesh axis runs over, the one named last changes fastest.
Arguments:
- features: bfloat16 [4096, 256], P(('row', 'rep')), may hold values from -6 to 6
- weight: bfloat16 [256, 256], replicated, may hold values from -0.375 to 0.375
- cotangent: bfloat16 [4096, 256], P(('row', 'rep')), may hold values from -6 to 6
- adjacency: bfloat16 [8, 4, 24, 128, 128], P('row', 'rep'), may hold values from -0.15625 to 0.15625
- tile_out: int32 [8, 4, 24], P('row', 'rep'), may hold values from 0 to 3
- tile_in: int32 [8, 4, 24], P('row', 'rep'), may hold values from 0 to 7
- live_count: int32 [8, 4], P('row', 'rep'), may hold values from 6 to 24, as said below
Outputs:
- activated: bfloat16 [4096, 256], P(('row', 'rep'))
- weight_grad: float32 [256, 256], replicated
- feature_grad: float32 [4096, 256], P(('row', 'rep'))
Inputs may be any that keep to these rules, and one draw needn't show every extreme that they name: `live_count`: live tile slots of one device; some device has all 24 slots live in every draw.
All inputs are finite; a program needn't handle non-finite values.
Results may differ from a plain program's by a relative error of at most 0.02.
Values may be sent and summed in bfloat16 or wider, within the bound.
A program may use at most 64 MiB of HBM per device.

v0:
```python
import math
import jax
import jax.numpy as jnp
from jax import lax
from jax.sharding import PartitionSpec as P


def tile_sums(adjacency, first_ids, second_ids, live_mask, table, count, transpose_tile):
    slot_count = adjacency.shape[0]
    block_rows = adjacency.shape[1]
    feat_width = table.shape[2]
    group_size = math.gcd(slot_count, 8)
    turns = slot_count // group_size
    items = (
        adjacency.reshape(turns, group_size, block_rows, block_rows),
        first_ids.reshape(turns, group_size),
        second_ids.reshape(turns, group_size),
        live_mask.reshape(turns, group_size),
    )

    def step_group(running, item):
        tile_group, read_ids, write_ids, live_group = item
        inputs = table[read_ids]
        if transpose_tile:
            products = jnp.einsum(
                "gji,gjf->gif", tile_group, inputs, preferred_element_type=jnp.float32
            )
        else:
            products = jnp.einsum(
                "gij,gjf->gif", tile_group, inputs, preferred_element_type=jnp.float32
            )
        onehot = (write_ids[None, :] == jnp.arange(count)[:, None]).astype(
            jnp.float32
        ) * live_group[None, :]
        running = running + jnp.einsum(
            "bg,gif->bif", onehot, products, precision=lax.Precision.HIGHEST
        )
        return (running, None)

    start = jnp.zeros((count, block_rows, feat_width), jnp.float32)
    running, unused = lax.scan(step_group, start, items)
    return running.reshape(count * block_rows, feat_width)


def add_sources(received):
    return jnp.sum(received.astype(jnp.float32), axis=0)


def body(features, weight, cotangent, adjacency, tile_out, tile_in, live_count):
    block_rows = features.shape[0]
    feat_width = features.shape[1]
    row_count = lax.axis_size("row")
    rep_count = lax.axis_size("rep")
    slot_count = adjacency.shape[2]
    adjacency = adjacency.reshape(slot_count, block_rows, block_rows)
    out_ids = tile_out.reshape(slot_count)
    in_ids = tile_in.reshape(slot_count)
    live_mask = (jnp.arange(slot_count) < live_count.reshape(())).astype(jnp.float32)
    gathered = lax.all_gather(features, "row", axis=0, tiled=True).reshape(
        row_count, block_rows, feat_width
    )
    partial_value = tile_sums(adjacency, in_ids, out_ids, live_mask, gathered, rep_count, False)
    aggregated = lax.psum_scatter(
        partial_value.astype(jnp.bfloat16), "rep", scatter_dimension=0, tiled=True
    )
    pre = jnp.dot(aggregated, weight, preferred_element_type=jnp.float32)
    sig = jax.nn.sigmoid(pre)
    activated = (pre * sig).astype(jnp.bfloat16)
    grad_pre = (cotangent.astype(jnp.float32) * sig * (1.0 + pre * (1.0 - sig))).astype(
        jnp.bfloat16
    )
    weight_part = jnp.dot(aggregated.T, grad_pre, preferred_element_type=jnp.float32)
    grad_rows = jnp.dot(grad_pre, weight.T, preferred_element_type=jnp.float32).astype(jnp.bfloat16)
    group_grads = lax.all_gather(grad_rows, "rep", axis=0, tiled=True)
    weight_grad = lax.psum(weight_part, ("row", "rep"))
    group_grads = group_grads.reshape(rep_count, block_rows, feat_width)
    returned = tile_sums(adjacency, out_ids, in_ids, live_mask, group_grads, row_count, True)
    rounded = returned.astype(jnp.bfloat16).reshape(row_count, block_rows, feat_width)
    feature_grad = add_sources(
        lax.all_to_all(rounded, "row", split_axis=0, concat_axis=0, tiled=True)
    )
    return (activated, weight_grad, feature_grad)


def solution(mesh):
    return jax.shard_map(
        body,
        mesh=mesh,
        in_specs=(
            P(("row", "rep"), None),
            P(),
            P(("row", "rep"), None),
            P("row", "rep", None, None, None),
            P("row", "rep", None),
            P("row", "rep", None),
            P("row", "rep"),
        ),
        out_specs=(P(("row", "rep"), None), P(), P(("row", "rep"), None)),
        check_vma=False,
    )
```

profile of v0, /device:TPU:0, one launch (start us, length us, event | category | flops | bytes accessed | tf_op | source)
XLA Modules:
  0.0 231.4 jit_solution(6620039171133740857)
XLA Ops:
  7.2 0.0 copy-start
  7.2 0.0 reduce-scatter.2.cloned.1.call-start
  7.9 0.0 copy-start.4
  7.9 0.5 broadcast.99
  8.4 0.1 copy-done.4
  8.6 0.7 reduce.6
  9.3 0.7 reduce.7
  9.9 0.1 reshape_reshape.14
  10.0 0.1 reshape_reshape.12
  10.1 16.7 %all_gather.6 = bf16[1024,256]{1,0:T(8,128)(2,1)S(1)} all-gather(bf16[128,256]{1,0:T(8,128)(2,1)} %param.11), channel_id=1, replica_groups=mesh['row'=8,'rep'=4] {'row'}, dimensions={0}, use_global_device_ids=true | all-gather | bytes 589824 | tf_op jit(solution)/shard_map/all_gather | solution.py:59
  26.8 10.8 %while.22 = (s32[]{:T(128)}, f32[4,128,256]{2,0,1:T(4,128)S(1)}, s32[3,8]{1,0:T(4,128)S(1)}, f32[3,8]{1,0:T(4,128)S(1)}, bf16[3,8,128,128]{3,2,1,0:T(8,128)(2,1)...) while((s32[]{:T(128)}, f32[4,128,256]{2,0,1:T(4,128)S(1)}, ...), condition=%wide.region_1.2_spmd.clone, body=%wide.region_0.1_spmd.clone.sunk | while | flops 79955032 | bytes 4985279 | solution.py:41
  26.8 0.6 gather_fusion
  27.4 1.2 fusion.61
  28.7 1.7 convolution_add_fusion.4
  30.5 0.6 gather_fusion
  31.0 1.2 fusion.61
  32.3 1.7 convolution_add_fusion.4
  34.1 0.6 gather_fusion
  34.7 1.2 fusion.61
  35.9 1.7 convolution_add_fusion.4
  37.6 0.0 copy-start.1
  37.6 0.8 copy.25
  38.4 0.0 reduce-scatter.2.cloned.1.call-update
  38.4 0.4 copy-done.1
  38.8 0.4 copy.13
  39.2 24.8 %reduce-scatter.2.cloned.1.call-done = bf16[128,256]{1,0:T(8,128)(2,1)} async-done(((bf16[512,256]{1,0:T(8,128)(2,1)}), bf16[128,256]{1,0:T(8,128)(2,1)}) %reduce-scatter.2.cloned.1.call-update) | async-done | bytes 65552 | tf_op jit(solution)/shard_map/reduce_scatter | solution.py:63
  64.0 1.7 multiply_convert_fusion
  65.7 0.2 convolution_convert_fusion
  65.9 9.3 %all_gather.7 = bf16[512,256]{1,0:T(8,128)(2,1)S(1)} all-gather(bf16[128,256]{1,0:T(8,128)(2,1)S(1)} %convolution_convert_fusion), channel_id=1, replica_groups=mesh['row'=8,'rep'=4] {'rep'}, dimensions={0}, use_global_device_ids=true | all-gather | bytes 327680 | tf_op jit(solution)/shard_map/all_gather | solution.py:74
  75.2 7.9 %while.23 = (s32[]{:T(128)}, f32[8,128,256]{2,0,1:T(8,128)S(1)}, s32[3,8]{1,0:T(4,128)S(1)}, f32[3,8]{1,0:T(4,128)S(1)}, bf16[3,8,128,128]{2,3,1,0:T(8,128)(2,1)...) while((s32[]{:T(128)}, f32[8,128,256]{2,0,1:T(8,128)S(1)}, ...), condition=%wide.region_5.6_spmd.clone, body=%wide.region_4.5_spmd.clone.sunk | while | flops 92800152 | bytes 6033855 | solution.py:41
  75.3 0.6 gather_fusion.1
  75.8 0.3 fusion.69
  76.1 1.7 convolution_add_fusion.5
  77.9 0.6 gather_fusion.1
  78.5 0.3 fusion.69
  78.8 1.7 convolution_add_fusion.5
  80.6 0.6 gather_fusion.1
  81.1 0.3 fusion.69
  81.4 1.7 convolution_add_fusion.5
  83.1 1.1 copy.24
  84.2 4.8 %all-to-all-start = ((bf16[8,128,256]{2,1,0:T(8,128)(2,1)}), bf16[8,128,256]{2,1,0:T(8,128)(2,1)S(1)}, u32[]{:S(2)}, u32[]{:S(2)}) async-start(bf16[8,128,256]{2,1,0:T(8,128)(2,1)} %copy.24), calls=%async_computation.1 | async-start | bytes 1048576 | tf_op jit(solution)/shard_map/all_to_all | solution.py:80
  89.0 0.0 all-reduce.2.cloned.1.call-start
  89.0 0.9 fusion.31
  89.9 0.0 all-reduce.2.cloned.1.call-update
  90.0 14.4 %all-to-all-done = bf16[8,128,256]{2,1,0:T(8,128)(2,1)S(1)} async-done(((bf16[8,128,256]{2,1,0:T(8,128)(2,1)}), bf16[8,128,256]{2,1,0:T(8,128)(2,1)S(1)}, u32[]{:S(2)}, u32[]{:S(2)}) %all-to-all-start) | async-done | bytes 524320 | tf_op jit(solution)/shard_map/all_to_all | solution.py:80
  104.3 0.7 convert_reduce_fusion
  105.1 117.8 %all-reduce.2.cloned.1.call-done = f32[256,256]{1,0:T(8,128)} async-done(((f32[256,256]{1,0:T(8,128)}), f32[256,256]{1,0:T(8,128)}) %all-reduce.2.cloned.1.call-update) | async-done | bytes 262160 | tf_op jit(solution)/shard_map/psum | solution.py:75
  222.9 1.7 copy.44
  (34 shorter events, 0.2 us)
Async XLA Ops:
  7.2 56.8 %copy-start = (bf16[256,256]{1,0:T(8,128)(2,1)S(1)}, bf16[256,256]{1,0:T(8,128)(2,1)}, u32[]{:S(2)}) copy-start(bf16[256,256]{1,0:T(8,128)(2,1)} %param.12) | copy-start | bytes 393220
  7.2 56.8 %reduce-scatter.2.cloned.1.call-start = ((), (), s32[]{:S(2)}) async-start(), calls=%async_computation.2 | async-start | bytes 327680 | tf_op jit(solution)/shard_map/reduce_scatter | solution.py:63
  7.9 0.7 copy-start.4
  8.6 0.7 copy-start.5
  37.6 1.2 copy-start.1
  38.8 25.2 %copy-start.3 = (bf16[128,256]{1,0:T(8,128)(2,1)S(1)}, bf16[128,256]{1,0:T(8,128)(2,1)}, u32[]{:S(2)}) copy-start(bf16[128,256]{1,0:T(8,128)(2,1)} %param.13) | copy-start | bytes 196612
  84.2 4.8 %copy-start.2 = (bf16[128,256]{1,0:T(8,128)(2,1)S(1)}, bf16[128,256]{1,0:T(8,128)(2,1)}, u32[]{:S(2)}) copy-start(bf16[128,256]{1,0:T(8,128)(2,1)} %reduce-scatter.2.cloned.1.call-done) | copy-start | bytes 196612
  84.2 20.1 %all-to-all-start = ((bf16[8,128,256]{2,1,0:T(8,128)(2,1)}), bf16[8,128,256]{2,1,0:T(8,128)(2,1)S(1)}, u32[]{:S(2)}, u32[]{:S(2)}) async-start(bf16[8,128,256]{2,1,0:T(8,128)(2,1)} %copy.24), calls=%async_computation.1 | async-start | bytes 1048576 | tf_op jit(solution)/shard_map/all_to_all | solution.py:80
  89.0 133.9 %all-reduce.2.cloned.1.call-start = ((), (), s32[]{:S(2)}) async-start(), calls=%async_computation.3 | async-start | bytes 524288 | tf_op jit(solution)/shard_map/psum | solution.py:75
Sparse Core Ops, SparseCore 0:
  38.5 25.4 reduce-scatter.1
  95.9 126.9 all-reduce.1
where the time goes:
time: 232 us; the launch traced here: 231 us
  waiting for transfers between devices  157 us (68%)
  blocking collectives  26 us (11%)
  matrix products  17.5 us (8%)
  between operations  14.8 us (6%)
  local copies, waits for them, and re-layouts  8.77 us (4%)
  starting transfers between devices  4.83 us (2%)
    psum x1, waiting for transfers between devices, body(): weight_grad = lax.psum(weight_part, ('row', 'rep'))  118 us
    reduce_scatter x1, waiting for transfers between devices, body(): lax.psum_scatter(partial_value.astype(jnp.bfloat16), 'rep', scatter_dimen...  24.8 us
    all_gather x1, blocking collectives, body(): lax.all_gather(features, 'row', axis=0, tiled=True)  16.7 us
    all_to_all x1, waiting for transfers between devices, body(): lax.all_to_all(rounded, 'row', split_axis=0, concat_axis=0, tiled=True)  14.4 us
    dot_general x6, matrix products, step_group(): jnp.einsum('bg,gif->bif', onehot, products, precision=lax.Precision.HIGHEST)  10.2 us
    all_gather x1, blocking collectives, body(): group_grads = lax.all_gather(grad_rows, 'rep', axis=0, tiled=True)  9.29 us
    all_to_all x1, starting transfers between devices, body(): lax.all_to_all(rounded, 'row', split_axis=0, concat_axis=0, tiled=True)  4.75 us
  transfers between devices with their start and end apart: 3, of which 3 were waited for; matrix products, arithmetic and copies ran while one was open for 1% of the time, Pallas kernels for 0%

commit v1 on v0

--- a/solution.py
+++ b/solution.py
@@ -72,7 +72,7 @@
     weight_part = jnp.dot(aggregated.T, grad_pre, preferred_element_type=jnp.float32)
     grad_rows = jnp.dot(grad_pre, weight.T, preferred_element_type=jnp.float32).astype(jnp.bfloat16)
     group_grads = lax.all_gather(grad_rows, "rep", axis=0, tiled=True)
-    weight_grad = lax.psum(weight_part, ("row", "rep"))
+    weight_grad = lax.psum(lax.psum(weight_part, "rep"), "row")
     group_grads = group_grads.reshape(rep_count, block_rows, feat_width)
     returned = tile_sums(adjacency, out_ids, in_ids, live_mask, group_grads, row_count, True)
     rounded = returned.astype(jnp.bfloat16).reshape(row_count, block_rows, feat_width)

time: 232 us -> 203 us (0.88)
  waiting for transfers between devices: 157 us -> 129 us
    all_to_all x1, waiting for transfers between devices: 14.4 us -> 0.01 us  [body(): lax.all_to_all(rounded, 'row', split_axis=0, concat_axis=0, tiled=True)]
    psum x1 -> x2, waiting for transfers between devices: 118 us -> 104 us  [body(): weight_grad = lax.psum(lax.psum(weight_part, 'rep'), 'row')]
  transfers between devices with their start and end apart: 3 -> 4, of which waited for: 3 -> 3; matrix products, arithmetic and copies ran while one was open for 1% -> 1% of each run, Pallas kernels for 0% -> 0%
where the time goes in v1:
time: 203 us
  waiting for transfers between devices  129 us (64%)
  blocking collectives  26 us (13%)
  matrix products  17.5 us (9%)
  between operations  14.5 us (7%)
  local copies, waits for them, and re-layouts  8.77 us (4%)
  starting transfers between devices  4.87 us (2%)
  other arithmetic  2.17 us (1%)
    psum x2, waiting for transfers between devices, body(): weight_grad = lax.psum(lax.psum(weight_part, 'rep'), 'row')  104 us
    reduce_scatter x1, waiting for transfers between devices, body(): lax.psum_scatter(partial_value.astype(jnp.bfloat16), 'rep', scatter_dimen...  24.8 us
    all_gather x1, blocking collectives, body(): lax.all_gather(features, 'row', axis=0, tiled=True)  16.7 us
    dot_general x6, matrix products, step_group(): jnp.einsum('bg,gif->bif', onehot, products, precision=lax.Precision.HIGHEST)  10.2 us
    all_gather x1, blocking collectives, body(): group_grads = lax.all_gather(grad_rows, 'rep', axis=0, tiled=True)  9.29 us
    all_to_all x1, starting transfers between devices, body(): lax.all_to_all(rounded, 'row', split_axis=0, concat_axis=0, tiled=True)  4.75 us
  transfers between devices with their start and end apart: 4, of which 3 were waited for; matrix products, arithmetic and copies ran while one was open for 1% of the time, Pallas kernels for 0%

profile of v1, /device:TPU:0, one launch (start us, length us, event | category | flops | bytes accessed | tf_op | source)
XLA Modules:
  0.0 202.8 jit_solution(15856842576006587616)
XLA Ops:
  7.2 0.0 copy-start
  7.2 0.0 reduce-scatter.2.cloned.1.call-start
  7.9 0.5 broadcast.99
  8.4 0.1 copy-done.4
  8.6 0.7 reduce.6
  9.3 0.7 reduce.7
  9.9 0.1 reshape_reshape.14
  10.0 0.1 reshape_reshape.12
  10.1 16.7 %all_gather.6 = bf16[1024,256]{1,0:T(8,128)(2,1)S(1)} all-gather(bf16[128,256]{1,0:T(8,128)(2,1)} %param.11), channel_id=1, replica_groups=mesh['row'=8,'rep'=4] {'row'}, dimensions={0}, use_global_device_ids=true | all-gather | bytes 589824 | tf_op jit(solution)/shard_map/all_gather | solution.py:59
  26.8 10.8 %while.22 = (s32[]{:T(128)}, f32[4,128,256]{2,0,1:T(4,128)S(1)}, s32[3,8]{1,0:T(4,128)S(1)}, f32[3,8]{1,0:T(4,128)S(1)}, bf16[3,8,128,128]{3,2,1,0:T(8,128)(2,1)...) while((s32[]{:T(128)}, f32[4,128,256]{2,0,1:T(4,128)S(1)}, ...), condition=%wide.region_1.2_spmd.clone, body=%wide.region_0.1_spmd.clone.sunk | while | flops 79955032 | bytes 4985279 | solution.py:41
  26.8 0.6 gather_fusion
  27.4 1.2 fusion.61
  28.7 1.7 convolution_add_fusion.4
  30.5 0.6 gather_fusion
  31.0 1.2 fusion.61
  32.3 1.7 convolution_add_fusion.4
  34.1 0.6 gather_fusion
  34.7 1.2 fusion.61
  35.9 1.7 convolution_add_fusion.4
  37.6 0.8 copy.25
  38.4 0.0 reduce-scatter.2.cloned.1.call-update
  38.4 0.4 copy-done.1
  38.8 0.4 copy.13
  39.2 24.8 %reduce-scatter.2.cloned.1.call-done = bf16[128,256]{1,0:T(8,128)(2,1)} async-done(((bf16[512,256]{1,0:T(8,128)(2,1)}), bf16[128,256]{1,0:T(8,128)(2,1)}) %reduce-scatter.2.cloned.1.call-update) | async-done | bytes 65552 | tf_op jit(solution)/shard_map/reduce_scatter | solution.py:63
  64.0 1.7 multiply_convert_fusion
  65.7 0.2 convolution_convert_fusion
  65.9 9.3 %all_gather.7 = bf16[512,256]{1,0:T(8,128)(2,1)S(1)} all-gather(bf16[128,256]{1,0:T(8,128)(2,1)S(1)} %convolution_convert_fusion), channel_id=1, replica_groups=mesh['row'=8,'rep'=4] {'rep'}, dimensions={0}, use_global_device_ids=true | all-gather | bytes 327680 | tf_op jit(solution)/shard_map/all_gather | solution.py:74
  75.2 7.9 %while.23 = (s32[]{:T(128)}, f32[8,128,256]{2,0,1:T(8,128)S(1)}, s32[3,8]{1,0:T(4,128)S(1)}, f32[3,8]{1,0:T(4,128)S(1)}, bf16[3,8,128,128]{2,3,1,0:T(8,128)(2,1)...) while((s32[]{:T(128)}, f32[8,128,256]{2,0,1:T(8,128)S(1)}, ...), condition=%wide.region_6.7_spmd.clone, body=%wide.region_5.6_spmd.clone.sunk | while | flops 92800152 | bytes 6033855 | solution.py:41
  75.3 0.6 gather_fusion.1
  75.8 0.3 fusion.69
  76.1 1.7 convolution_add_fusion.5
  77.9 0.6 gather_fusion.1
  78.5 0.3 fusion.69
  78.8 1.7 convolution_add_fusion.5
  80.6 0.6 gather_fusion.1
  81.1 0.3 fusion.69
  81.4 1.7 convolution_add_fusion.5
  83.1 1.1 copy.24
  84.2 4.8 %all-to-all-start = ((bf16[8,128,256]{2,1,0:T(8,128)(2,1)}), bf16[8,128,256]{2,1,0:T(8,128)(2,1)S(1)}, u32[]{:S(2)}, u32[]{:S(2)}) async-start(bf16[8,128,256]{2,1,0:T(8,128)(2,1)} %copy.24), calls=%async_computation.1 | async-start | bytes 1048576 | tf_op jit(solution)/shard_map/all_to_all | solution.py:80
  89.0 0.0 all-reduce.3.cloned.1.call-start
  89.0 0.9 fusion.31
  89.9 0.0 all-reduce.3.cloned.1.call-update
  90.0 0.0 all-reduce.5.cloned.1.call-start
  90.0 46.8 %all-reduce.3.cloned.1.call-done = f32[256,256]{1,0:T(8,128)} async-done(((f32[256,256]{1,0:T(8,128)}), f32[256,256]{1,0:T(8,128)}) %all-reduce.3.cloned.1.call-update) | async-done | bytes 262160 | tf_op jit(solution)/shard_map/psum | solution.py:75
  136.8 0.0 all-reduce.5.cloned.1.call-update
  136.9 0.7 convert_reduce_fusion
  137.6 57.0 %all-reduce.5.cloned.1.call-done = f32[256,256]{1,0:T(8,128)} async-done(((f32[256,256]{1,0:T(8,128)}), f32[256,256]{1,0:T(8,128)}) %all-reduce.5.cloned.1.call-update) | async-done | bytes 262160 | tf_op jit(solution)/shard_map/psum | solution.py:75
  194.6 1.7 copy.45
  (37 shorter events, 0.2 us)
Async XLA Ops:
  7.2 56.8 %copy-start = (bf16[256,256]{1,0:T(8,128)(2,1)S(1)}, bf16[256,256]{1,0:T(8,128)(2,1)}, u32[]{:S(2)}) copy-start(bf16[256,256]{1,0:T(8,128)(2,1)} %param.12) | copy-start | bytes 393220
  7.2 56.8 %reduce-scatter.2.cloned.1.call-start = ((), (), s32[]{:S(2)}) async-start(), calls=%async_computation.2 | async-start | bytes 327680 | tf_op jit(solution)/shard_map/reduce_scatter | solution.py:63
  7.9 0.7 copy-start.4
  8.6 0.7 copy-start.5
  37.6 1.2 copy-start.1
  38.8 25.2 %copy-start.3 = (bf16[128,256]{1,0:T(8,128)(2,1)S(1)}, bf16[128,256]{1,0:T(8,128)(2,1)}, u32[]{:S(2)}) copy-start(bf16[128,256]{1,0:T(8,128)(2,1)} %param.13) | copy-start | bytes 196612
  84.2 4.8 %copy-start.2 = (bf16[128,256]{1,0:T(8,128)(2,1)S(1)}, bf16[128,256]{1,0:T(8,128)(2,1)}, u32[]{:S(2)}) copy-start(bf16[128,256]{1,0:T(8,128)(2,1)} %reduce-scatter.2.cloned.1.call-done) | copy-start | bytes 196612
  84.2 52.6 %all-to-all-start = ((bf16[8,128,256]{2,1,0:T(8,128)(2,1)}), bf16[8,128,256]{2,1,0:T(8,128)(2,1)S(1)}, u32[]{:S(2)}, u32[]{:S(2)}) async-start(bf16[8,128,256]{2,1,0:T(8,128)(2,1)} %copy.24), calls=%async_computation.1 | async-start | bytes 1048576 | tf_op jit(solution)/shard_map/all_to_all | solution.py:80
  89.0 47.9 %all-reduce.3.cloned.1.call-start = ((), (), s32[]{:S(2)}) async-start(), calls=%async_computation.3 | async-start | bytes 524288 | tf_op jit(solution)/shard_map/psum | solution.py:75
  90.0 104.6 %all-reduce.5.cloned.1.call-start = ((), (), s32[]{:S(2)}) async-start(), calls=%async_computation.4 | async-start | bytes 524288 | tf_op jit(solution)/shard_map/psum | solution.py:75
Sparse Core Ops, SparseCore 0:
  38.5 25.4 reduce-scatter.1
  93.3 43.5 all-reduce.2
  139.2 55.4 all-reduce.4
